TPU v7x, 256 devices: a whole 4x4x8 slice. The times are simulated.
256 devices in a mesh: col: 32 (over x, y, core), sub: 8 (over z).
Axes of the slice: x: 4, y: 4, z: 8, core: 2. Of those that a mesh axis runs over, the one named last changes fastest.
Arguments:
- vectors: bfloat16 [1048576, 128], P(('col', 'sub')), may hold values from -6 to 6
- near_blocks: bfloat16 [4096, 4, 256, 256], P(('col', 'sub')), may hold values from -0.1875 to 0.1875
- near_index: int32 [4096, 4], P(('col', 'sub')), may hold values from 0 to 4095, as said below
- leaf_basis: bfloat16 [4096, 32, 256], P(('col', 'sub')), may hold values from -0.375 to 0.375
- leaf_transfer: float32 [4096, 32, 32], P(('col', 'sub')), may hold values from -0.25 to 0.25
- leaf_coupling: float32 [4096, 8, 32, 32], P(('col', 'sub')), may hold values from -0.375 to 0.375
- leaf_far: int32 [4096, 8], P(('col', 'sub')), may hold values from 0 to 4095, as said below
- cluster_transfer: float32 [256, 32, 32], P(('col', 'sub')), may hold values from -0.375 to 0.375
- cluster_coupling: float32 [256, 4, 32, 32], P(('col', 'sub')), may hold values from -0.5 to 0.5
- cluster_partner: int32 [256, 4], P(('col', 'sub')), may hold values from 0 to 7
- top_coupling: float32 [32, 8, 32, 32], P('col'), may hold values from -0.375 to 0.375
- top_partner: int32 [32, 8], P('col'), may hold values from 0 to 31
Outputs:
- products: bfloat16 [1048576, 128], P(('col', 'sub'))
Inputs may be any that keep to these rules, and one draw needn't show every extreme that they name: `near_index`: slot 0 of leaf i is i itself; every entry lies within 16 leaves of i; slot 1 is exactly 16 leaves away from i. `leaf_far`: every entry lies within 16 leaves of its row leaf i; slots 0 and 1 are exactly 16 leaves away from i.
All inputs are finite; a program needn't handle non-finite values.
Results may differ from a plain program's by a relative error of at most 0.0034.
Values may be sent and summed in bfloat16 or wider, within the bound.
A program may use at most 64 MiB of HBM per device.

v0:
```python
import jax
import jax.numpy as jnp
from jax import lax
from jax.sharding import PartitionSpec as P

HIGHEST = lax.Precision.HIGHEST


def with_halo(block, sides, width):
    for axis, dim in sides:
        count = lax.axis_size(axis)
        forward = [(i, i + 1) for i in range(count - 1)]
        backward = [(target, source) for source, target in forward]
        low = lax.ppermute(
            lax.slice_in_dim(block, block.shape[dim] - width, None, axis=dim), axis, forward
        )
        high = lax.ppermute(lax.slice_in_dim(block, 0, width, axis=dim), axis, backward)
        block = jnp.concatenate([low, block, high], axis=dim)
    return block


def local(
    vectors,
    near_blocks,
    near_index,
    leaf_basis,
    leaf_transfer,
    leaf_coupling,
    leaf_far,
    cluster_transfer,
    cluster_coupling,
    cluster_partner,
    top_coupling,
    top_partner,
):
    leaves_here = leaf_basis.shape[0]
    leaf_rows = leaf_basis.shape[2]
    columns = vectors.shape[1]
    window_start = lax.axis_index(("col", "sub")) * leaves_here - leaves_here
    widened = with_halo(vectors, ((("col", "sub"), 0),), leaves_here * leaf_rows)
    window_vec = widened.reshape(3 * leaves_here, leaf_rows, columns)
    own_vec = vectors.reshape(leaves_here, leaf_rows, columns)
    leaf_coefs = jnp.einsum("lrp,lpc->lrc", leaf_basis, own_vec, preferred_element_type=jnp.float32)
    window_coefs = with_halo(leaf_coefs, ((("col", "sub"), 0),), leaves_here)
    cluster_coef = jnp.einsum("lrs,lrc->sc", leaf_transfer, leaf_coefs, precision=HIGHEST)
    sub_coefs = lax.all_gather(cluster_coef[None], "sub", axis=0, tiled=True)
    cluster_field = jnp.einsum(
        "krs,ksc->rc", cluster_coupling[0], sub_coefs[cluster_partner[0]], precision=HIGHEST
    )
    upward = jnp.dot(cluster_transfer[0].T, cluster_coef, precision=HIGHEST)
    top_coef = lax.psum(upward, "sub")
    col_coefs = lax.all_gather(top_coef[None], "col", axis=0, tiled=True)
    top_field = jnp.einsum(
        "krs,ksc->rc", top_coupling[0], col_coefs[top_partner[0]], precision=HIGHEST
    )
    cluster_field = cluster_field + jnp.dot(cluster_transfer[0], top_field, precision=HIGHEST)
    far_coefs = window_coefs[leaf_far - window_start]
    leaf_field = jnp.einsum("lkrs,lksc->lrc", leaf_coupling, far_coefs, precision=HIGHEST)
    leaf_field = leaf_field + jnp.einsum(
        "lrs,sc->lrc", leaf_transfer, cluster_field, precision=HIGHEST
    )
    rounded = leaf_field.astype(jnp.bfloat16)
    picked = window_vec[near_index - window_start]
    near_part = jnp.einsum(
        "lkij,lkjc->lic", near_blocks, picked, preferred_element_type=jnp.float32
    )
    far_part = jnp.einsum("lrp,lrc->lpc", leaf_basis, rounded, preferred_element_type=jnp.float32)
    return (near_part + far_part).astype(jnp.bfloat16).reshape(leaves_here * leaf_rows, columns)


def solution(mesh):
    in_specs = (
        P(("col", "sub"), None),
        P(("col", "sub"), None, None, None),
        P(("col", "sub"), None),
        P(("col", "sub"), None, None),
        P(("col", "sub"), None, None),
        P(("col", "sub"), None, None, None),
        P(("col", "sub"), None),
        P(("col", "sub"), None, None),
        P(("col", "sub"), None, None, None),
        P(("col", "sub"), None),
        P("col", None, None, None),
        P("col", None),
    )
    out_specs = P(("col", "sub"), None)
    return jax.shard_map(local, mesh=mesh, in_specs=in_specs, out_specs=out_specs, check_vma=False)
```

profile of v0, /device:TPU:1, one launch (start us, length us, event | category | flops | bytes accessed | tf_op | source)
XLA Modules:
  0.0 154.2 jit_solution(7868082268854348627)
XLA Ops:
  0.0 1.7 %fusion.12 = f32[16,32,128]{2,1,0:T(8,128)S(1)} fusion(bf16[16,32,256]{2,1,0:T(8,128)(2,1)} %param.15, bf16[16,256,128]{2,1,0:T(8,128)(2,1)} %bitcast.79), kind=kOutput, calls=%fused_computation.33 | convolution fusion | flops 33554432 | bytes 1572864 | tf_op jit(solution)/shard_map/lrp,lpc->lrc/dot_general | solution.py:43
  1.7 8.9 %collective-permute-start.3 = (f32[16,32,128]{2,1,0:T(8,128)S(1)}, f32[16,32,128]{2,1,0:T(8,128)S(1)}, u32[]{:S(2)}, u32[]{:S(2)}) collective-permute-start(f32[16,32,128]{2,1,0:T(8,128)S(1)} %fusion.12), channel_id=1, source_target_pairs={{1,0},{2,1},{3,2},{4,3},{5,4},{6,5},{7,6},{8,7},{9,8},{10,9},{11,1... | collective-permute-start | bytes 786440 | tf_op jit(solution)/shard_map/ppermute | solution.py:17
  10.6 1.9 %collective-permute-start.2 = (f32[16,32,128]{2,1,0:T(8,128)S(1)}, f32[16,32,128]{2,1,0:T(8,128)}, u32[]{:S(2)}, u32[]{:S(2)}) collective-permute-start(f32[16,32,128]{2,1,0:T(8,128)S(1)} %fusion.12), channel_id=1, source_target_pairs={{0,1},{1,2},{2,3},{3,4},{4,5},{5,6},{6,7},{7,8},{8,9},{9,10},{10,1... | collective-permute-start | bytes 786440 | tf_op jit(solution)/shard_map/ppermute | solution.py:14
  12.5 4.9 %collective-permute-start.1 = (bf16[4096,128]{1,0:T(8,128)(2,1)}, bf16[4096,128]{1,0:T(8,128)(2,1)}, u32[]{:S(2)}, u32[]{:S(2)}) collective-permute-start(bf16[4096,128]{1,0:T(8,128)(2,1)} %param.12), channel_id=1, source_target_pairs={{1,0},{2,1},{3,2},{4,3},{5,4},{6,5},{7,6},{8,7},{9,8},{10,9},{11,1... | collective-permute-start | bytes 3145736 | tf_op jit(solution)/shard_map/ppermute | solution.py:17
  17.4 1.9 %collective-permute-start = (bf16[4096,128]{1,0:T(8,128)(2,1)}, bf16[4096,128]{1,0:T(8,128)(2,1)}, u32[]{:S(2)}, u32[]{:S(2)}) collective-permute-start(bf16[4096,128]{1,0:T(8,128)(2,1)} %param.12), channel_id=1, source_target_pairs={{0,1},{1,2},{2,3},{3,4},{4,5},{5,6},{6,7},{7,8},{8,9},{9,10},{10,1... | collective-permute-start | bytes 3145736 | tf_op jit(solution)/shard_map/ppermute | solution.py:14
  19.3 0.7 fusion.10
  20.0 0.7 fusion.11
  20.7 1.3 compare_select_fusion.1
  21.9 0.7 compare_select_fusion
  22.6 0.6 pad_clamp_fusion
  23.3 0.6 reshape.78
  23.9 1.5 fusion.13
  25.4 0.9 convolution_bitcast_fusion.3
  26.4 35.0 %psum.7 = f32[1,32,128]{2,1,0:T(8,128)S(1)} all-reduce(f32[1,32,128]{2,1,0:T(8,128)S(1)} %convolution_bitcast_fusion.3), channel_id=1, replica_groups=mesh['col'=32,'sub'=8] {'sub'}, use_global_device_ids=true, to_apply=%region_0.0 | all-reduce | flops 4096 | bytes 32768 | tf_op jit(solution)/shard_map/psum | solution.py:51
  61.4 18.5 %all-gather = f32[256,128]{1,0:T(8,128)S(1)} all-gather(f32[32,128]{1,0:T(8,128)S(1)} %bitcast.81), channel_id=2, replica_groups=mesh['col'=32,'sub'=8] {'sub'}, dimensions={0}, use_global_device_ids=true | all-gather | bytes 147456 | tf_op jit(solution)/shard_map/all_gather | solution.py:46
  79.9 36.2 %all_gather.7 = f32[32,32,128]{2,1,0:T(8,128)S(1)} all-gather(f32[1,32,128]{2,1,0:T(8,128)S(1)} %psum.7), channel_id=1, replica_groups=mesh['col'=32,'sub'=8] {'col'}, dimensions={0}, use_global_device_ids=true | all-gather | bytes 540672 | tf_op jit(solution)/shard_map/all_gather | solution.py:52
  116.1 0.6 gather_fusion.2
  116.6 0.2 convolution_bitcast_fusion.4
  116.9 0.7 gather_fusion.3
  117.6 0.3 convolution_bitcast_fusion.2
  117.9 0.6 pad_clamp_fusion.2
  118.5 0.7 copy.22
  119.4 0.9 fusion.4
  120.3 1.0 pad_maximum_fusion.1
  121.3 2.1 %gather_fusion.1 = f32[128,32,128]{2,1,0:T(8,128)} fusion(f32[48,32,128]{2,1,0:T(8,128)S(1)} %pad_maximum_fusion.1, s32[1024]{0:T(1024)S(1)} %pad_clamp_fusion.2), kind=kCustom, calls=%fused_computation.1 | custom fusion | bytes 4194816 | tf_op jit(solution)/shard_map/gather | solution.py:57
  123.4 4.4 %convolution_bitcast_fusion.1 = f32[16,32,128]{2,1,0:T(8,128)S(1)} fusion(f32[16,8,32,128]{3,2,1,0:T(8,128)} %bitcast.78, f32[16,8,32,32]{3,2,1,0:T(8,128)S(1)} %copy-done), kind=kOutput, calls=%fused_computation.10 | convolution fusion | flops 201326592 | bytes 2883584 | tf_op jit(solution)/shard_map/lkrs,lksc->lrc/dot_general | solution.py:58
  127.9 0.4 fusion.3
  128.2 1.9 %fusion.14 = f32[16,128,256]{2,1,0:T(8,128)} fusion(bf16[16,32,128]{2,1,0:T(8,128)(2,1)S(1)} %fusion.3, bf16[16,32,256]{2,1,0:T(8,128)(2,1)S(1)} %copy-done.2), kind=kOutput, calls=%fused_computation.35 | convolution fusion | flops 33554432 | bytes 2490368 | tf_op jit(solution)/shard_map/lrp,lrc->lpc/dot_general | solution.py:67
  130.1 9.8 %pad_maximum_fusion = bf16[12288,128]{1,0:T(8,128)(2,1)} fusion(bf16[4096,128]{1,0:T(8,128)(2,1)} %collective-permute-done.1, bf16[4096,128]{1,0:T(8,128)(2,1)S(1)} %copy-done.1, bf16[4096,128]{1,0:T(8,128)(2,1)} %collective-permute-done), kind=kLoop, calls=%fused_computation.4 | loop fusion | flops 9437184 | bytes 6291456 | tf_op jit(solution)/shard_map/concatenate | solution.py:18
  139.9 4.9 %gather_fusion = bf16[64,256,128]{2,1,0:T(8,128)(2,1)} fusion(bf16[48,256,128]{2,1,0:T(8,128)(2,1)} %bitcast.76, s32[1024]{0:T(1024)S(1)} %pad_clamp_fusion.3), kind=kCustom, calls=%fused_computation | custom fusion | bytes 8388864 | tf_op jit(solution)/shard_map/gather | solution.py:63
  144.8 8.1 %fusion.1 = bf16[16,256,128]{1,2,0:T(8,128)(2,1)S(1)} fusion(f32[16,128,256]{2,1,0:T(8,128)} %fusion.14, bf16[16,4,256,128]{3,2,1,0:T(8,128)(2,1)} %bitcast.77, bf16[16,4,256,256]{3,2,1,0:T(8,128)(2,1)} %param.13), kind=kOutput, calls=%fused_computation.7 | convolution fusion | flops 1074790400 | bytes 15728640 | tf_op jit(solution)/shard_map/lkij,lkjc->lic/dot_general | solution.py:64
  152.9 1.3 copy.26
  (20 shorter events, 0.2 us)
Async XLA Ops:
  0.0 123.4 %copy-start = (f32[16,8,32,32]{3,2,1,0:T(8,128)S(1)}, f32[16,8,32,32]{3,2,1,0:T(8,128)}, u32[]{:S(2)}) copy-start(f32[16,8,32,32]{3,2,1,0:T(8,128)} %param.17) | copy-start | bytes 1572868
  0.0 116.6 %copy-start.5 = (f32[1,4,32,32]{3,2,1,0:T(8,128)S(1)}, f32[1,4,32,32]{3,2,1,0:T(8,128)}, u32[]{:S(2)}) copy-start(f32[1,4,32,32]{3,2,1,0:T(8,128)} %param.20) | copy-start | bytes 49156
  0.0 117.6 %copy-start.4 = (f32[1,8,32,32]{3,2,1,0:T(8,128)S(1)}, f32[1,8,32,32]{3,2,1,0:T(8,128)}, u32[]{:S(2)}) copy-start(f32[1,8,32,32]{3,2,1,0:T(8,128)} %param.22) | copy-start | bytes 98308
  1.7 118.5 %collective-permute-start.3 = (f32[16,32,128]{2,1,0:T(8,128)S(1)}, f32[16,32,128]{2,1,0:T(8,128)S(1)}, u32[]{:S(2)}, u32[]{:S(2)}) collective-permute-start(f32[16,32,128]{2,1,0:T(8,128)S(1)} %fusion.12), channel_id=1, source_target_pairs={{1,0},{2,1},{3,2},{4,3},{5,4},{6,5},{7,6},{8,7},{9,8},{10,9},{11,1... | collective-permute-start | bytes 786440 | tf_op jit(solution)/shard_map/ppermute | solution.py:17
  10.6 109.6 %collective-permute-start.2 = (f32[16,32,128]{2,1,0:T(8,128)S(1)}, f32[16,32,128]{2,1,0:T(8,128)}, u32[]{:S(2)}, u32[]{:S(2)}) collective-permute-start(f32[16,32,128]{2,1,0:T(8,128)S(1)} %fusion.12), channel_id=1, source_target_pairs={{0,1},{1,2},{2,3},{3,4},{4,5},{5,6},{6,7},{7,8},{8,9},{9,10},{10,1... | collective-permute-start | bytes 786440 | tf_op jit(solution)/shard_map/ppermute | solution.py:14
  12.5 117.6 %collective-permute-start.1 = (bf16[4096,128]{1,0:T(8,128)(2,1)}, bf16[4096,128]{1,0:T(8,128)(2,1)}, u32[]{:S(2)}, u32[]{:S(2)}) collective-permute-start(bf16[4096,128]{1,0:T(8,128)(2,1)} %param.12), channel_id=1, source_target_pairs={{1,0},{2,1},{3,2},{4,3},{5,4},{6,5},{7,6},{8,7},{9,8},{10,9},{11,1... | collective-permute-start | bytes 3145736 | tf_op jit(solution)/shard_map/ppermute | solution.py:17
  17.4 112.7 %collective-permute-start = (bf16[4096,128]{1,0:T(8,128)(2,1)}, bf16[4096,128]{1,0:T(8,128)(2,1)}, u32[]{:S(2)}, u32[]{:S(2)}) collective-permute-start(bf16[4096,128]{1,0:T(8,128)(2,1)} %param.12), channel_id=1, source_target_pairs={{0,1},{1,2},{2,3},{3,4},{4,5},{5,6},{6,7},{7,8},{8,9},{9,10},{10,1... | collective-permute-start | bytes 3145736 | tf_op jit(solution)/shard_map/ppermute | solution.py:14
  123.4 4.4 %copy-start.3 = (f32[16,32,32]{2,1,0:T(8,128)S(1)}, f32[16,32,32]{2,1,0:T(8,128)}, u32[]{:S(2)}) copy-start(f32[16,32,32]{2,1,0:T(8,128)} %param.16) | copy-start | bytes 196612
  123.4 4.8 %copy-start.2 = (bf16[16,32,256]{2,1,0:T(8,128)(2,1)S(1)}, bf16[16,32,256]{2,1,0:T(8,128)(2,1)}, u32[]{:S(2)}) copy-start(bf16[16,32,256]{2,1,0:T(8,128)(2,1)} %param.15) | copy-start | bytes 786436
  123.4 6.7 %copy-start.1 = (bf16[4096,128]{1,0:T(8,128)(2,1)S(1)}, bf16[4096,128]{1,0:T(8,128)(2,1)}, u32[]{:S(2)}) copy-start(bf16[4096,128]{1,0:T(8,128)(2,1)} %param.12) | copy-start | bytes 3145732
where the time goes:
time: 155 us; the launch traced here: 154 us
  blocking collectives  89.7 us (58%)
  matrix products  20.3 us (13%)
  starting transfers between devices  17.6 us (11%)
  other arithmetic  15.3 us (10%)
  local copies, waits for them, and re-layouts  11.1 us (7%)
    all_gather x1, blocking collectives, local(): col_coefs = lax.all_gather(top_coef[None], 'col', axis=0, tiled=True)  36.2 us
    psum x1, blocking collectives, local(): top_coef = lax.psum(upward, 'sub')  35 us
    all_gather x1, blocking collectives, local(): sub_coefs = lax.all_gather(cluster_coef[None], 'sub', axis=0, tiled=True)  18.5 us
    ppermute x2, starting transfers between devices, with_halo(): lax.ppermute(lax.slice_in_dim(block, 0, width, axis=dim), axis, backward)  13.7 us
    concatenate x2, other arithmetic, with_halo(): block = jnp.concatenate([low, block, high], axis=dim)  10.8 us
    dot_general x1, matrix products, local(): jnp.einsum('lkij,lkjc->lic', near_blocks, picked, preferred_element_type=...  8.06 us
    gather x1, local copies, waits for them, and re-layouts, local(): picked = window_vec[near_index - window_start]  4.91 us
    dot_general x1, matrix products, local(): jnp.einsum('lkrs,lksc->lrc', leaf_coupling, far_coefs, precision=HIGHEST)  4.43 us
  transfers between devices with their start and end apart: 4, of which 0 were waited for; matrix products, arithmetic and copies ran while one was open for 14% of the time, Pallas kernels for 0%

commit v1 on v0

v1 whole, which is shorter than its diff:
```python
import functools

import jax
import jax.numpy as jnp
from jax import lax
from jax.experimental import pallas as pl
from jax.experimental.pallas import tpu as pltpu
from jax.sharding import PartitionSpec as P

MESH = pl.DeviceIdType.MESH
BF = jnp.bfloat16
F32 = jnp.float32


def matmul(a, b):
    return jnp.dot(a, b, preferred_element_type=F32)


def matmul_t(a, b):
    return lax.dot_general(a, b, (((0,), (0,)), ((), ())), preferred_element_type=F32)


def kernel(
    n_col,
    n_sub,
    first,
    vec,
    near_blocks,
    near_index,
    leaf_basis,
    leaf_transfer,
    leaf_coupling,
    leaf_far,
    cluster_transfer,
    cluster_coupling,
    cluster_partner,
    top_coupling,
    top_partner,
    out,
    own,
    win_a,
    win_b,
    blocks,
    basis,
    transfer,
    coupling,
    c_transfer,
    c_coupling,
    t_coupling,
    coefs,
    cwin,
    zsend,
    zbuf,
    tsend,
    tbuf,
    acc,
    local_sem,
    block_sem,
    bulk_send,
    bulk_recv,
    coef_send,
    coef_recv,
    z_send,
    z_recv,
    t_send,
    t_recv,
):
    leaves, rows, cols = own.shape
    near = blocks.shape[1]
    far0 = coupling.shape[1]
    rank = basis.shape[1]
    half = rows // 2
    col = lax.axis_index("col")
    sub = lax.axis_index("sub")
    here = col * n_sub + sub
    total = n_col * n_sub
    window_start = (here - 1) * leaves

    def device(index):
        return (index // n_sub, lax.rem(index, n_sub))

    def within(leaf):
        return jnp.minimum(jnp.maximum(leaf - window_start, 0), 3 * leaves - 1)

    following = device(lax.rem(here + 1, total))
    previous = device(lax.rem(here + total - 1, total))

    loads = [
        pltpu.make_async_copy(vec, own, local_sem.at[0]),
        pltpu.make_async_copy(leaf_basis, basis, local_sem.at[1]),
        pltpu.make_async_copy(leaf_transfer, transfer, local_sem.at[2]),
        pltpu.make_async_copy(cluster_transfer, c_transfer, local_sem.at[3]),
        pltpu.make_async_copy(cluster_coupling, c_coupling, local_sem.at[4]),
        pltpu.make_async_copy(top_coupling, t_coupling, local_sem.at[5]),
        pltpu.make_async_copy(vec.at[:, pl.ds(0, half)], win_a.at[pl.ds(leaves, leaves)], local_sem.at[6]),
        pltpu.make_async_copy(vec.at[:, pl.ds(half, half)], win_b.at[pl.ds(leaves, leaves)], local_sem.at[7]),
        pltpu.make_async_copy(leaf_coupling, coupling, local_sem.at[8]),
    ]
    for load in loads:
        load.start()
    block_load = pltpu.make_async_copy(near_blocks, blocks, block_sem)
    block_load.start()

    barrier = pltpu.get_barrier_semaphore()
    for target in (following, previous):
        pl.semaphore_signal(barrier, inc=1, device_id=target, device_id_type=MESH)

    def greet_sub(j, carry):
        pl.semaphore_signal(barrier, inc=1, device_id=(col, lax.rem(sub + j, n_sub)), device_id_type=MESH)
        return carry

    def greet_col(j, carry):
        pl.semaphore_signal(barrier, inc=1, device_id=(lax.rem(col + j, n_col), sub), device_id_type=MESH)
        return carry

    lax.fori_loop(1, n_sub, greet_sub, 0)
    lax.fori_loop(1, n_col, greet_col, 0)
    pl.semaphore_wait(barrier, 2 + (n_sub - 1) + (n_col - 1))

    def bulk(number, window, row, start, count):
        source = vec.at[pl.ds(start, count), pl.ds(row, half)]
        return [
            pltpu.make_async_remote_copy(
                src_ref=source,
                dst_ref=window.at[pl.ds(start, count)],
                send_sem=bulk_send.at[2 * number],
                recv_sem=bulk_recv.at[2 * number],
                device_id=following,
                device_id_type=MESH,
            ),
            pltpu.make_async_remote_copy(
                src_ref=source,
                dst_ref=window.at[pl.ds(2 * leaves + start, count)],
                send_sem=bulk_send.at[2 * number + 1],
                recv_sem=bulk_recv.at[2 * number + 1],
                device_id=previous,
                device_id_type=MESH,
            ),
        ]

    part_a = bulk(0, win_a, 0, 0, first) + bulk(1, win_a, 0, first, leaves - first)
    part_b = bulk(2, win_b, half, 0, leaves)
    for copy in part_a[:2]:
        copy.start()

    for load in loads[:3]:
        load.wait()

    for leaf in range(leaves):
        value = matmul(basis[leaf], own[leaf])
        coefs[leaf] = value.astype(BF)
        cwin[leaves + leaf] = value.astype(BF)
    for load in loads[3:6]:
        load.wait()
    cluster_coef = matmul_t(
        transfer[...].reshape(leaves * rank, rank).astype(BF), coefs[...].reshape(leaves * rank, cols)
    ).astype(BF)
    upward = matmul_t(c_transfer[0].astype(BF), cluster_coef)
    zsend[0] = cluster_coef
    zsend[1] = upward.astype(BF)
    z_copies = [
        pltpu.make_async_remote_copy(
            src_ref=zsend,
            dst_ref=zbuf.at[sub],
            send_sem=z_send.at[j],
            recv_sem=z_recv.at[j],
            device_id=(col, lax.rem(sub + j, n_sub)),
            device_id_type=MESH,
        )
        for j in range(1, n_sub)
    ]
    for copy in z_copies:
        copy.start()
    coef_copies = [
        pltpu.make_async_remote_copy(
            src_ref=coefs,
            dst_ref=cwin.at[pl.ds(2 * leaves * side, leaves)],
            send_sem=coef_send.at[side],
            recv_sem=coef_recv.at[side],
            device_id=target,
            device_id_type=MESH,
        )
        for side, target in enumerate((following, previous))
    ]
    for copy in coef_copies:
        copy.start()
    for copy in part_a[2:] + part_b:
        copy.start()

    keep_z = pltpu.make_async_copy(zsend, zbuf.at[sub], local_sem.at[9])
    keep_z.start()
    keep_z.wait()
    for copy in z_copies:
        copy.wait()

    top = zbuf[0, 1].astype(F32)
    for s in range(1, n_sub):
        top = top + zbuf[s, 1].astype(F32)
    tsend[...] = top.astype(BF)

    def top_copy(j):
        return pltpu.make_async_remote_copy(
            src_ref=tsend,
            dst_ref=tbuf.at[col],
            send_sem=t_send.at[j],
            recv_sem=t_recv.at[j],
            device_id=(lax.rem(col + j, n_col), sub),
            device_id_type=MESH,
        )

    def start_top(j, carry):
        top_copy(j).start()
        return carry

    def wait_top(j, carry):
        top_copy(j).wait()
        return carry

    lax.fori_loop(1, n_col, start_top, 0)
    keep_t = pltpu.make_async_copy(tsend, tbuf.at[col], local_sem.at[9])
    keep_t.start()

    cluster_field = jnp.zeros((rank, cols), F32)
    for k in range(c_coupling.shape[1]):
        cluster_field = cluster_field + matmul(c_coupling[0, k].astype(BF), zbuf[cluster_partner[0, k], 0])

    block_load.wait()

    def own_product(leaf, carry):
        acc[leaf] = matmul(blocks[leaf, 0], own[leaf])
        return carry

    lax.fori_loop(0, leaves, own_product, 0)

    keep_t.wait()
    lax.fori_loop(1, n_col, wait_top, 0)
    top_field = jnp.zeros((rank, cols), F32)
    for k in range(t_coupling.shape[1]):
        top_field = top_field + matmul(t_coupling[0, k].astype(BF), tbuf[top_partner[0, k]])
    cluster_field = cluster_field + matmul(c_transfer[0].astype(BF), top_field.astype(BF))
    parent = cluster_field.astype(BF)

    for load in loads[6:]:
        load.wait()
    for copy in coef_copies:
        copy.wait()

    def far_product(leaf, carry):
        field = matmul(transfer[leaf].astype(BF), parent)
        for k in range(far0):
            field = field + matmul(coupling[leaf, k].astype(BF), cwin[within(leaf_far[k, leaf])])
        acc[leaf] += matmul_t(basis[leaf], field.astype(BF))
        return carry

    lax.fori_loop(0, leaves, far_product, 0)

    def near_sum(leaf, window, start):
        index = [within(near_index[k, leaf]) for k in range(1, near)]
        left = jnp.concatenate([blocks[leaf, k, :, start : start + half] for k in range(1, near)], axis=1)
        right = jnp.concatenate([window[i] for i in index], axis=0)
        return acc[leaf] + matmul(left, right)

    for copy in part_a:
        copy.wait()

    def near_first(leaf, carry):
        acc[leaf] = near_sum(leaf, win_a, 0)
        return carry

    lax.fori_loop(0, leaves, near_first, 0)
    for copy in part_b:
        copy.wait()

    def near_second(leaf, carry):
        out[leaf] = near_sum(leaf, win_b, half).astype(BF)
        return carry

    lax.fori_loop(0, leaves, near_second, 0)


def local(n_col, n_sub, *args):
    (
        vectors,
        near_blocks,
        near_index,
        leaf_basis,
        leaf_transfer,
        leaf_coupling,
        leaf_far,
        cluster_transfer,
        cluster_coupling,
        cluster_partner,
        top_coupling,
        top_partner,
    ) = args
    leaves, rank, rows = leaf_basis.shape
    cols = vectors.shape[1]
    half = rows // 2
    anywhere = pl.BlockSpec(memory_space=pl.ANY)
    scalars = pl.BlockSpec(memory_space=pltpu.SMEM)
    dma = pltpu.SemaphoreType.DMA
    out = pl.pallas_call(
        functools.partial(kernel, n_col, n_sub, 4),
        out_shape=jax.ShapeDtypeStruct((leaves, rows, cols), BF),
        in_specs=[
            anywhere,
            anywhere,
            scalars,
            anywhere,
            anywhere,
            anywhere,
            scalars,
            anywhere,
            anywhere,
            scalars,
            anywhere,
            scalars,
        ],
        out_specs=pl.BlockSpec(memory_space=pltpu.VMEM),
        scratch_shapes=[
            pltpu.VMEM((leaves, rows, cols), BF),
            pltpu.VMEM((3 * leaves, half, cols), BF),
            pltpu.VMEM((3 * leaves, half, cols), BF),
            pltpu.VMEM(near_blocks.shape, BF),
            pltpu.VMEM(leaf_basis.shape, BF),
            pltpu.VMEM(leaf_transfer.shape, F32),
            pltpu.VMEM(leaf_coupling.shape, F32),
            pltpu.VMEM(cluster_transfer.shape, F32),
            pltpu.VMEM(cluster_coupling.shape, F32),
            pltpu.VMEM(top_coupling.shape, F32),
            pltpu.VMEM((leaves, rank, cols), BF),
            pltpu.VMEM((3 * leaves, rank, cols), BF),
            pltpu.VMEM((2, rank, cols), BF),
            pltpu.VMEM((n_sub, 2, rank, cols), BF),
            pltpu.VMEM((rank, cols), BF),
            pltpu.VMEM((n_col, rank, cols), BF),
            pltpu.VMEM((leaves, rows, cols), F32),
            dma((10,)),
            dma,
            dma((6,)),
            dma((6,)),
            dma((2,)),
            dma((2,)),
            dma((n_sub,)),
            dma((n_sub,)),
            dma((n_col,)),
            dma((n_col,)),
        ],
        compiler_params=pltpu.CompilerParams(collective_id=0, has_side_effects=True),
    )(
        vectors.reshape(leaves, rows, cols),
        near_blocks,
        near_index.T,
        leaf_basis,
        leaf_transfer,
        leaf_coupling,
        leaf_far.T,
        cluster_transfer,
        cluster_coupling,
        cluster_partner,
        top_coupling,
        top_partner,
    )
    return out.reshape(leaves * rows, cols)


def solution(mesh):
    leaf = ("col", "sub")
    in_specs = (
        P(leaf, None),
        P(leaf, None, None, None),
        P(leaf, None),
        P(leaf, None, None),
        P(leaf, None, None),
        P(leaf, None, None, None),
        P(leaf, None),
        P(leaf, None, None),
        P(leaf, None, None, None),
        P(leaf, None),
        P("col", None, None, None),
        P("col", None),
    )
    body = functools.partial(local, mesh.shape["col"], mesh.shape["sub"])
    return jax.shard_map(body, mesh=mesh, in_specs=in_specs, out_specs=P(leaf, None), check_vma=False)
```

time: 155 us -> 50.8 us (0.33)
  blocking collectives: 89.7 us -> 0 us
  Pallas kernels: 0 us -> 48.3 us
  matrix products: 20.3 us -> 0 us
  starting transfers between devices: 17.6 us -> 0 us
  other arithmetic: 15.3 us -> 0 us
  local copies, waits for them, and re-layouts: 11.1 us -> 2.26 us
    all_gather x2 -> x0, blocking collectives: 54.7 us -> none  [the longest x1 36.2 us: local(): col_coefs = lax.all_gather(top_coef[None], 'col', axis=0, tiled=True)]
    pallas_call x0 -> x1, Pallas kernels: none -> 48.3 us  [local(): pl.pallas_call(functools.partial(kernel, n_col, n_sub, 4), out_shape=jax....]
    psum x1 -> x0, blocking collectives: 35 us -> none  [local(): top_coef = lax.psum(upward, 'sub')]
    dot_general x10 -> x0, matrix products: 20.3 us -> none  [the longest x1 8.06 us: local(): jnp.einsum('lkij,lkjc->lic', near_blocks, picked, preferred_element_type=...]
    ppermute x4 -> x0, starting transfers between devices: 17.6 us -> none  [the longest x2 13.7 us: with_halo(): lax.ppermute(lax.slice_in_dim(block, 0, width, axis=dim), axis, backward)]
    concatenate x2 -> x0, other arithmetic: 10.8 us -> none  [with_halo(): block = jnp.concatenate([low, block, high], axis=dim)]
    gather x4 -> x0, local copies, waits for them, and re-layouts: 8.28 us -> none  [the longest x1 4.91 us: local(): picked = window_vec[near_index - window_start]]
    select_n x4 -> x0, other arithmetic: 3.27 us -> none  [the longest x1 1.26 us: local(): picked = window_vec[near_index - window_start]]
  transfers between devices with their start and end apart: 4 -> 0, of which waited for: 0 -> 0; matrix products, arithmetic and copies ran while one was open for 14% -> 0% of each run, Pallas kernels for 0% -> 0%
where the time goes in v1:
time: 50.8 us; the launch traced here: 50.6 us
  Pallas kernels  48.3 us (95%)
  local copies, waits for them, and re-layouts  2.26 us (4%)
    pallas_call x1, Pallas kernels, local(): pl.pallas_call(functools.partial(kernel, n_col, n_sub, 4), out_shape=jax....  48.3 us
    unnamed x1, local copies, waits for them, and re-layouts  2.26 us

profile of v1, /device:TPU:1, one launch (start us, length us, event | category | flops | bytes accessed | tf_op | source)
XLA Modules:
  0.0 50.6 jit_solution(5138082595153808798)
XLA Ops:
  0.0 48.3 %shard_map.118 = bf16[16,256,128]{2,1,0:T(8,128)(2,1)} custom-call(bf16[16,256,128]{2,1,0:T(8,128)(2,1)} %bitcast.5, bf16[16,4,256,256]{3,2,1,0:T(8,128)(2,1)} %near_blocks.1, s32[4,16]{1,0:T(4,128)} %bitcast.7, bf16[16,32,256]{2,1,0:T(8,128)(2,1)} %leaf_basis.1, f32[16,32,32]{2,1,0:T(8,128)} %leaf_transfer.1, f32[16,8,32,32]{3,2,1,0:T(8,128)} %leaf_coupling.1, ...), custom_call_target="tpu_custom_call" | custom-call | tf_op jit(solution)/shard_map/pallas_call | solution.py:302
  48.4 2.3 %copy.14 = bf16[4096,128]{1,0:T(8,128)(2,1)} copy(bf16[4096,128]{1,0:T(8,128)(2,1)} %bitcast.4) | data formatting | bytes 2097152

commit v2 on v1

v2 whole, which is shorter than its diff:
```python
import functools

import jax
import jax.numpy as jnp
from jax import lax
from jax.experimental import pallas as pl
from jax.experimental.pallas import tpu as pltpu
from jax.sharding import PartitionSpec as P

MESH = pl.DeviceIdType.MESH
BF = jnp.bfloat16
F32 = jnp.float32


def matmul(a, b):
    return jnp.dot(a, b, preferred_element_type=F32)


def matmul_t(a, b):
    return lax.dot_general(a, b, (((0,), (0,)), ((), ())), preferred_element_type=F32)


def kernel(
    n_col,
    n_sub,
    first,
    vec,
    near_blocks,
    near_index,
    leaf_basis,
    leaf_transfer,
    leaf_coupling,
    leaf_far,
    cluster_transfer,
    cluster_coupling,
    cluster_partner,
    top_coupling,
    top_partner,
    out,
    own,
    win_a,
    win_b,
    blocks,
    packed,
    basis,
    transfer,
    coupling,
    c_transfer,
    c_coupling,
    t_coupling,
    coefs,
    cwin,
    zsend,
    zbuf,
    tsend,
    tbuf,
    field,
    acc,
    load_sem,
    bulk_send,
    bulk_recv,
    coef_send,
    coef_recv,
    z_send,
    z_recv,
    t_send,
    t_recv,
    known,
):
    leaves, rows, cols = own.shape
    near = blocks.shape[1]
    far0 = coupling.shape[1]
    rank = basis.shape[1]
    rows_a, rows_b = win_a.shape[1], win_b.shape[1]
    col = lax.axis_index("col")
    sub = lax.axis_index("sub")
    here = col * n_sub + sub
    total = n_col * n_sub
    window_start = (here - 1) * leaves
    has_next = here < total - 1
    has_prev = here > 0

    def within(leaf):
        return jnp.minimum(jnp.maximum(leaf - window_start, 0), 3 * leaves - 1)

    def device(index):
        return (index // n_sub, lax.rem(index, n_sub))

    following = device(lax.rem(here + 1, total))
    previous = device(lax.rem(here + total - 1, total))

    def at_col(step):
        return (lax.rem(col + step + n_col, n_col), sub)

    def at_sub(step):
        return (col, lax.rem(sub + step + n_sub, n_sub))

    def signal(sem, target):
        pl.semaphore_signal(sem, inc=1, device_id=target, device_id_type=MESH)

    barrier = pltpu.get_barrier_semaphore()
    signal(barrier, at_col(-1))

    @pl.when(has_prev)
    def _():
        signal(barrier, previous)

    @pl.when(sub == 0)
    def _():
        signal(barrier, at_sub(-1))

    own_load = pltpu.make_async_copy(vec, own, load_sem.at[0])
    basis_load = pltpu.make_async_copy(leaf_basis, basis, load_sem.at[1])
    transfer_loads = [
        pltpu.make_async_copy(leaf_transfer, transfer, load_sem.at[2]),
        pltpu.make_async_copy(cluster_transfer, c_transfer, load_sem.at[3]),
    ]
    block_load = pltpu.make_async_copy(near_blocks, blocks, load_sem.at[4])
    coupling_load = pltpu.make_async_copy(leaf_coupling, coupling, load_sem.at[5])
    window_loads = [
        pltpu.make_async_copy(vec.at[:, pl.ds(0, rows_a)], win_a.at[pl.ds(leaves, leaves)], load_sem.at[6]),
        pltpu.make_async_copy(vec.at[:, pl.ds(rows_a, rows_b)], win_b.at[pl.ds(leaves, leaves)], load_sem.at[7]),
    ]
    tree_loads = [
        pltpu.make_async_copy(cluster_coupling, c_coupling, load_sem.at[8]),
        pltpu.make_async_copy(top_coupling, t_coupling, load_sem.at[9]),
    ]
    for load in [own_load, basis_load] + transfer_loads:
        load.start()

    greeted = 1 + jnp.where(has_next, 1, 0) + jnp.where(sub == n_sub - 1, 1, 0)
    pl.semaphore_wait(barrier, greeted)

    def onward(number, source, window, send_sem, recv_sem):
        return pltpu.make_async_remote_copy(
            src_ref=source,
            dst_ref=window,
            send_sem=send_sem.at[number],
            recv_sem=recv_sem.at[number],
            device_id=following,
            device_id_type=MESH,
        )

    def backward(number, source, window, send_sem, recv_sem):
        return pltpu.make_async_remote_copy(
            src_ref=source,
            dst_ref=window,
            send_sem=send_sem.at[number],
            recv_sem=recv_sem.at[number],
            device_id=previous,
            device_id_type=MESH,
        )

    parts = [(win_a, 0, rows_a, 0, first), (win_a, 0, rows_a, first, leaves - first), (win_b, rows_a, rows_b, 0, leaves)]
    up, down = [], []
    for number, (window, row, height, start, count) in enumerate(parts):
        source = vec.at[pl.ds(start, count), pl.ds(row, height)]
        up.append(onward(2 * number, source, window.at[pl.ds(start, count)], bulk_send, bulk_recv))
        down.append(
            backward(2 * number + 1, source, window.at[pl.ds(2 * leaves + start, count)], bulk_send, bulk_recv)
        )
    coef_up = onward(0, coefs, cwin.at[pl.ds(0, leaves)], coef_send, coef_recv)
    coef_down = backward(1, coefs, cwin.at[pl.ds(2 * leaves, leaves)], coef_send, coef_recv)

    def start_up(copies):
        @pl.when(has_next)
        def _():
            for copy in copies:
                copy.start()

    def start_down(copies):
        @pl.when(has_prev)
        def _():
            for copy in copies:
                copy.start()

    def finish(up_copies, down_copies):
        @pl.when(has_next)
        def _():
            for copy in up_copies:
                copy.wait_send()
            for copy in down_copies:
                copy.wait_recv()

        @pl.when(has_prev)
        def _():
            for copy in up_copies:
                copy.wait_recv()
            for copy in down_copies:
                copy.wait_send()

    start_up(up[:1])

    signal(known.at[0], at_col(1))

    @pl.when(has_next)
    def _():
        signal(known.at[1], following)

    @pl.when(sub == n_sub - 1)
    def _():
        signal(known.at[2], at_sub(1))

    @pl.when(has_prev)
    def _():
        pl.semaphore_wait(known.at[1], 1)

    start_down(down[:1])

    @pl.when(sub == 0)
    def _():
        pl.semaphore_wait(known.at[2], 1)

    pl.semaphore_wait(known.at[0], 1)

    def tell(number, targets):
        for target in targets:
            signal(known.at[number], target)

    tell(3, (at_sub(1), at_sub(-1)))
    tell(4, (at_col(1), at_col(-1)))

    for load in window_loads + [block_load]:
        load.start()

    own_load.wait()
    basis_load.wait()
    for leaf in range(leaves):
        value = matmul(basis[leaf], own[leaf]).astype(BF)
        coefs[leaf] = value
        cwin[leaves + leaf] = value

    pl.semaphore_wait(known.at[3], 2)
    tell(5, (at_sub(2), at_sub(-2)))
    pl.semaphore_wait(known.at[4], 2)
    tell(6, (at_col(2), at_col(-2)))

    for load in transfer_loads:
        load.wait()
    cluster_coef = matmul_t(
        transfer[...].reshape(leaves * rank, rank).astype(BF), coefs[...].reshape(leaves * rank, cols)
    )
    zsend[0:rank] = cluster_coef.astype(BF)
    tall = rank * rank // cols
    zsend[rank : rank + tall] = jnp.concatenate(
        [c_transfer[0, tall * q : tall * (q + 1)] for q in range(rank // tall)], axis=1
    ).astype(BF)

    pl.semaphore_wait(known.at[5], 2)
    z_copies = [
        pltpu.make_async_remote_copy(
            src_ref=zsend,
            dst_ref=zbuf.at[sub],
            send_sem=z_send.at[j],
            recv_sem=z_recv.at[j],
            device_id=at_sub(j),
            device_id_type=MESH,
        )
        for j in range(1, n_sub)
    ]
    for copy in z_copies:
        copy.start()
    start_up([coef_up] + up[1:])
    start_down([coef_down] + down[1:])
    keep_z = pltpu.make_async_copy(zsend, zbuf.at[sub], load_sem.at[10])
    keep_z.start()
    for load in [coupling_load] + tree_loads:
        load.start()
    pl.semaphore_wait(known.at[6], 2)
    tell(7, (at_col(4), at_col(-4)))

    block_load.wait()

    def own_product(leaf, carry):
        acc[leaf] = matmul(blocks[leaf, 0], own[leaf])
        packed[leaf] = jnp.concatenate([blocks[leaf, k, :, rows_a:rows] for k in range(1, near)], axis=1)
        return carry

    lax.fori_loop(0, leaves // 2, own_product, 0)
    pl.semaphore_wait(known.at[7], 2)
    tell(8, (at_col(8), at_col(-8)))
    lax.fori_loop(leaves // 2, leaves, own_product, 0)

    keep_z.wait()
    for copy in z_copies:
        copy.wait()
    gathered = zbuf[...].astype(F32)
    top = jnp.zeros((rank, cols), F32)
    for q in range(rank // tall):
        left = gathered[:, rank : rank + tall, rank * q : rank * (q + 1)].reshape(n_sub * tall, rank)
        right = gathered[:, tall * q : tall * (q + 1)].reshape(n_sub * tall, cols)
        top = top + matmul_t(left.astype(BF), right.astype(BF))
    tsend[...] = top.astype(BF)

    def top_copy(j):
        return pltpu.make_async_remote_copy(
            src_ref=tsend,
            dst_ref=tbuf.at[col],
            send_sem=t_send.at[j],
            recv_sem=t_recv.at[j],
            device_id=at_col(j),
            device_id_type=MESH,
        )

    def start_top(j, carry):
        top_copy(j).start()
        return carry

    def wait_top(j, carry):
        top_copy(j).wait()
        return carry

    pl.semaphore_wait(known.at[8], 2)
    lax.fori_loop(1, n_col, start_top, 0)
    keep_t = pltpu.make_async_copy(tsend, tbuf.at[col], load_sem.at[10])
    keep_t.start()

    for load in [coupling_load] + tree_loads:
        load.wait()
    cluster_field = jnp.zeros((rank, cols), F32)
    for k in range(c_coupling.shape[1]):
        cluster_field = cluster_field + matmul(c_coupling[0, k].astype(BF), zbuf[cluster_partner[0, k], 0:rank])

    finish([coef_up], [coef_down])

    def far_sum(leaf, carry):
        left = jnp.concatenate([coupling[leaf, k] for k in range(far0)], axis=1).astype(BF)
        right = jnp.concatenate([cwin[within(leaf_far[k, leaf])] for k in range(far0)], axis=0)
        field[leaf] = matmul(left, right)
        return carry

    lax.fori_loop(0, leaves, far_sum, 0)

    keep_t.wait()
    lax.fori_loop(1, n_col, wait_top, 0)
    top_field = jnp.zeros((rank, cols), F32)
    for k in range(t_coupling.shape[1]):
        top_field = top_field + matmul(t_coupling[0, k].astype(BF), tbuf[top_partner[0, k]])
    cluster_field = cluster_field + matmul(c_transfer[0].astype(BF), top_field.astype(BF))
    parent = cluster_field.astype(BF)

    def far_product(leaf, carry):
        value = field[leaf] + matmul(transfer[leaf].astype(BF), parent)
        acc[leaf] += matmul_t(basis[leaf], value.astype(BF))
        return carry

    lax.fori_loop(0, leaves, far_product, 0)

    for load in window_loads:
        load.wait()
    finish(up[:2], down[:2])

    def near_first(leaf, carry):
        value = acc[leaf]
        for k in range(1, near):
            value = value + matmul(blocks[leaf, k, :, 0:rows_a], win_a[within(near_index[k, leaf])])
        acc[leaf] = value
        return carry

    lax.fori_loop(0, leaves, near_first, 0)
    finish(up[2:], down[2:])

    def near_second(leaf, carry):
        right = jnp.concatenate([win_b[within(near_index[k, leaf])] for k in range(1, near)], axis=0)
        out[leaf] = (acc[leaf] + matmul(packed[leaf], right)).astype(BF)
        return carry

    lax.fori_loop(0, leaves, near_second, 0, unroll=True)


def local(n_col, n_sub, *args):
    (
        vectors,
        near_blocks,
        near_index,
        leaf_basis,
        leaf_transfer,
        leaf_coupling,
        leaf_far,
        cluster_transfer,
        cluster_coupling,
        cluster_partner,
        top_coupling,
        top_partner,
    ) = args
    leaves, rank, rows = leaf_basis.shape
    near = near_blocks.shape[1]
    cols = vectors.shape[1]
    rows_b = rows // 4
    rows_a = rows - rows_b
    anywhere = pl.BlockSpec(memory_space=pl.ANY)
    scalars = pl.BlockSpec(memory_space=pltpu.SMEM)
    dma = pltpu.SemaphoreType.DMA
    out = pl.pallas_call(
        functools.partial(kernel, n_col, n_sub, 3),
        out_shape=pltpu.VMEM((leaves, rows, cols), BF),
        in_specs=[
            anywhere,
            anywhere,
            scalars,
            anywhere,
            anywhere,
            anywhere,
            scalars,
            anywhere,
            anywhere,
            scalars,
            anywhere,
            scalars,
        ],
        out_specs=pl.BlockSpec(memory_space=pltpu.VMEM),
        scratch_shapes=[
            pltpu.VMEM((leaves, rows, cols), BF),
            pltpu.VMEM((3 * leaves, rows_a, cols), BF),
            pltpu.VMEM((3 * leaves, rows_b, cols), BF),
            pltpu.VMEM(near_blocks.shape, BF),
            pltpu.VMEM((leaves, rows, (near - 1) * rows_b), BF),
            pltpu.VMEM(leaf_basis.shape, BF),
            pltpu.VMEM(leaf_transfer.shape, F32),
            pltpu.VMEM(leaf_coupling.shape, F32),
            pltpu.VMEM(cluster_transfer.shape, F32),
            pltpu.VMEM(cluster_coupling.shape, F32),
            pltpu.VMEM(top_coupling.shape, F32),
            pltpu.VMEM((leaves, rank, cols), BF),
            pltpu.VMEM((3 * leaves, rank, cols), BF),
            pltpu.VMEM((rank + rank * rank // cols, cols), BF),
            pltpu.VMEM((n_sub, rank + rank * rank // cols, cols), BF),
            pltpu.VMEM((rank, cols), BF),
            pltpu.VMEM((n_col, rank, cols), BF),
            pltpu.VMEM((leaves, rank, cols), F32),
            pltpu.VMEM((leaves, rows, cols), F32),
            dma((11,)),
            dma((6,)),
            dma((6,)),
            dma((2,)),
            dma((2,)),
            dma((n_sub,)),
            dma((n_sub,)),
            dma((n_col,)),
            dma((n_col,)),
            pltpu.SemaphoreType.REGULAR((9,)),
        ],
        compiler_params=pltpu.CompilerParams(collective_id=0, has_side_effects=True),
    )(
        vectors.reshape(leaves, rows, cols),
        near_blocks,
        near_index.T,
        leaf_basis,
        leaf_transfer,
        leaf_coupling,
        leaf_far.T,
        cluster_transfer,
        cluster_coupling,
        cluster_partner,
        top_coupling,
        top_partner,
    )
    return out.reshape(leaves * rows, cols)


def solution(mesh):
    leaf = ("col", "sub")
    in_specs = (
        P(leaf, None),
        P(leaf, None, None, None),
        P(leaf, None),
        P(leaf, None, None),
        P(leaf, None, None),
        P(leaf, None, None, None),
        P(leaf, None),
        P(leaf, None, None),
        P(leaf, None, None, None),
        P(leaf, None),
        P("col", None, None, None),
        P("col", None),
    )
    body = functools.partial(local, mesh.shape["col"], mesh.shape["sub"])
    return jax.shard_map(body, mesh=mesh, in_specs=in_specs, out_specs=P(leaf, None), check_vma=False)
```

time: 50.8 us -> 41.7 us (0.82)
  Pallas kernels: 48.3 us -> 40.6 us
  local copies, waits for them, and re-layouts: 2.26 us -> 0.97 us
    pallas_call x1, Pallas kernels: 48.3 us -> 40.6 us  [local(): pl.pallas_call(functools.partial(kernel, n_col, n_sub, 3), out_shape=pltp...]
    unnamed x1, local copies, waits for them, and re-layouts: 2.26 us -> 0.97 us
where the time goes in v2:
time: 41.7 us; the launch traced here: 41.6 us
  Pallas kernels  40.6 us (97%)
  local copies, waits for them, and re-layouts  0.97 us (2%)
    pallas_call x1, Pallas kernels, local(): pl.pallas_call(functools.partial(kernel, n_col, n_sub, 3), out_shape=pltp...  40.6 us
    unnamed x1, local copies, waits for them, and re-layouts  0.97 us

profile of v2, /device:TPU:1, one launch (start us, length us, event | category | flops | bytes accessed | tf_op | source)
XLA Modules:
  0.0 41.6 jit_solution(12588433785325952130)
XLA Ops:
  0.0 40.6 %shard_map.118 = bf16[16,256,128]{2,1,0:T(8,128)(2,1)S(1)} custom-call(bf16[16,256,128]{2,1,0:T(8,128)(2,1)} %bitcast.5, bf16[16,4,256,256]{3,2,1,0:T(8,128)(2,1)} %near_blocks.1, s32[4,16]{1,0:T(4,128)} %bitcast.7, bf16[16,32,256]{2,1,0:T(8,128)(2,1)} %leaf_basis.1, f32[16,32,32]{2,1,0:T(8,128)} %leaf_transfer.1, f32[16,8,32,32]{3,2,1,0:T(8,128)} %leaf_coupling.1, ...), custom_call_target="tpu_custom_call" | custom-call | tf_op jit(solution)/shard_map/pallas_call | solution.py:394
  40.7 1.0 %copy.14 = bf16[4096,128]{1,0:T(8,128)(2,1)} copy(bf16[4096,128]{1,0:T(8,128)(2,1)S(1)} %bitcast.4) | data formatting | bytes 2097152

commit v3 on v2

--- a/solution.py
+++ b/solution.py
@@ -1,4 +1,5 @@
 import functools
+import math
 
 import jax
 import jax.numpy as jnp
@@ -23,19 +24,20 @@
 def kernel(
     n_col,
     n_sub,
+    side,
     first,
     vec,
     near_blocks,
-    near_index,
+    near_table,
     leaf_basis,
     leaf_transfer,
     leaf_coupling,
-    leaf_far,
+    far_table,
     cluster_transfer,
     cluster_coupling,
-    cluster_partner,
+    cluster_table,
     top_coupling,
-    top_partner,
+    top_table,
     out,
     own,
     win_a,
@@ -66,6 +68,11 @@
     t_send,
     t_recv,
     known,
+    table_sem,
+    near_index,
+    leaf_far,
+    cluster_partner,
+    top_partner,
 ):
     leaves, rows, cols = own.shape
     near = blocks.shape[1]
@@ -92,6 +99,15 @@
     def at_col(step):
         return (lax.rem(col + step + n_col, n_col), sub)
 
+    def walk(position):
+        line, place = position // (2 * side), lax.rem(position, 2 * side)
+        chip, core = place // 2, lax.rem(place, 2)
+        odd = lax.rem(line, 2)
+        return line * 2 * side + (odd * (side - 1) + (1 - 2 * odd) * chip) * 2 + core
+
+    def along(step):
+        return (walk(lax.rem(walk(col) + step + n_col, n_col)), sub)
+
     def at_sub(step):
         return (col, lax.rem(sub + step + n_sub, n_sub))
 
@@ -99,7 +115,7 @@
         pl.semaphore_signal(sem, inc=1, device_id=target, device_id_type=MESH)
 
     barrier = pltpu.get_barrier_semaphore()
-    signal(barrier, at_col(-1))
+    signal(barrier, along(-1))
 
     @pl.when(has_prev)
     def _():
@@ -191,7 +207,7 @@
 
     start_up(up[:1])
 
-    signal(known.at[0], at_col(1))
+    signal(known.at[0], along(1))
 
     @pl.when(has_next)
     def _():
@@ -211,14 +227,11 @@
     def _():
         pl.semaphore_wait(known.at[2], 1)
 
-    pl.semaphore_wait(known.at[0], 1)
-
     def tell(number, targets):
         for target in targets:
             signal(known.at[number], target)
 
     tell(3, (at_sub(1), at_sub(-1)))
-    tell(4, (at_col(1), at_col(-1)))
 
     for load in window_loads + [block_load]:
         load.start()
@@ -232,8 +245,8 @@
 
     pl.semaphore_wait(known.at[3], 2)
     tell(5, (at_sub(2), at_sub(-2)))
-    pl.semaphore_wait(known.at[4], 2)
-    tell(6, (at_col(2), at_col(-2)))
+    pl.semaphore_wait(known.at[0], 1)
+    tell(4, (along(1), along(-1)))
 
     for load in transfer_loads:
         load.wait()
@@ -264,10 +277,16 @@
     start_down([coef_down] + down[1:])
     keep_z = pltpu.make_async_copy(zsend, zbuf.at[sub], load_sem.at[10])
     keep_z.start()
-    for load in [coupling_load] + tree_loads:
+    table_loads = [
+        pltpu.make_async_copy(source, target, table_sem.at[i])
+        for i, (source, target) in enumerate(
+            ((near_table, near_index), (far_table, leaf_far), (cluster_table, cluster_partner), (top_table, top_partner))
+        )
+    ]
+    for load in [coupling_load] + tree_loads + table_loads:
         load.start()
-    pl.semaphore_wait(known.at[6], 2)
-    tell(7, (at_col(4), at_col(-4)))
+    pl.semaphore_wait(known.at[4], 2)
+    tell(6, (along(2), along(-2)))
 
     block_load.wait()
 
@@ -277,9 +296,11 @@
         return carry
 
     lax.fori_loop(0, leaves // 2, own_product, 0)
+    pl.semaphore_wait(known.at[6], 2)
+    tell(7, (along(4), along(-4)))
+    lax.fori_loop(leaves // 2, leaves, own_product, 0)
     pl.semaphore_wait(known.at[7], 2)
-    tell(8, (at_col(8), at_col(-8)))
-    lax.fori_loop(leaves // 2, leaves, own_product, 0)
+    tell(8, (along(8), along(-8)))
 
     keep_z.wait()
     for copy in z_copies:
@@ -315,7 +336,7 @@
     keep_t = pltpu.make_async_copy(tsend, tbuf.at[col], load_sem.at[10])
     keep_t.start()
 
-    for load in [coupling_load] + tree_loads:
+    for load in [coupling_load] + tree_loads + table_loads:
         load.wait()
     cluster_field = jnp.zeros((rank, cols), F32)
     for k in range(c_coupling.shape[1]):
@@ -389,10 +410,10 @@
     rows_b = rows // 4
     rows_a = rows - rows_b
     anywhere = pl.BlockSpec(memory_space=pl.ANY)
-    scalars = pl.BlockSpec(memory_space=pltpu.SMEM)
+    scalars = anywhere
     dma = pltpu.SemaphoreType.DMA
     out = pl.pallas_call(
-        functools.partial(kernel, n_col, n_sub, 3),
+        functools.partial(kernel, n_col, n_sub, math.isqrt(n_col // 2), 4),
         out_shape=pltpu.VMEM((leaves, rows, cols), BF),
         in_specs=[
             anywhere,
@@ -439,6 +460,11 @@
             dma((n_col,)),
             dma((n_col,)),
             pltpu.SemaphoreType.REGULAR((9,)),
+            dma((4,)),
+            pltpu.SMEM((near, leaves), jnp.int32),
+            pltpu.SMEM((leaf_far.shape[1], leaves), jnp.int32),
+            pltpu.SMEM(cluster_partner.shape, jnp.int32),
+            pltpu.SMEM(top_partner.shape, jnp.int32),
         ],
         compiler_params=pltpu.CompilerParams(collective_id=0, has_side_effects=True),
     )(

time: 41.7 us -> 39.6 us (0.950)
  the two profiles are of different devices: /device:TPU:1 before, /device:TPU:3 now
where the time goes in v3:
time: 39.6 us; the launch traced here: 39.5 us
  Pallas kernels  38.5 us (97%)
  local copies, waits for them, and re-layouts  0.97 us (2%)
    pallas_call x1, Pallas kernels, local(): pl.pallas_call(functools.partial(kernel, n_col, n_sub, math.isqrt(n_col /...  38.5 us
    unnamed x1, local copies, waits for them, and re-layouts  0.97 us

profile of v3, /device:TPU:3, one launch (start us, length us, event | category | flops | bytes accessed | tf_op | source)
XLA Modules:
  0.0 39.5 jit_solution(16300026457169644595)
XLA Ops:
  0.0 38.5 %shard_map.118 = bf16[16,256,128]{2,1,0:T(8,128)(2,1)S(1)} custom-call(bf16[16,256,128]{2,1,0:T(8,128)(2,1)} %bitcast.5, bf16[16,4,256,256]{3,2,1,0:T(8,128)(2,1)} %near_blocks.1, s32[4,16]{1,0:T(4,128)} %bitcast.7, bf16[16,32,256]{2,1,0:T(8,128)(2,1)} %leaf_basis.1, f32[16,32,32]{2,1,0:T(8,128)} %leaf_transfer.1, f32[16,8,32,32]{3,2,1,0:T(8,128)} %leaf_coupling.1, ...), custom_call_target="tpu_custom_call" | custom-call | tf_op jit(solution)/shard_map/pallas_call | solution.py:415
  38.5 1.0 %copy.14 = bf16[4096,128]{1,0:T(8,128)(2,1)} copy(bf16[4096,128]{1,0:T(8,128)(2,1)S(1)} %bitcast.4) | data formatting | bytes 2097152

commit v4 on v3

--- a/solution.py
+++ b/solution.py
@@ -26,6 +26,7 @@
     n_sub,
     side,
     first,
+    more,
     vec,
     near_blocks,
     near_table,
@@ -167,7 +168,12 @@
             device_id_type=MESH,
         )
 
-    parts = [(win_a, 0, rows_a, 0, first), (win_a, 0, rows_a, first, leaves - first), (win_b, rows_a, rows_b, 0, leaves)]
+    parts = [
+        (win_a, 0, rows_a, 0, first),
+        (win_a, 0, rows_a, first, more),
+        (win_a, 0, rows_a, first + more, leaves - first - more),
+        (win_b, rows_a, rows_b, 0, leaves),
+    ]
     up, down = [], []
     for number, (window, row, height, start, count) in enumerate(parts):
         source = vec.at[pl.ds(start, count), pl.ds(row, height)]
@@ -205,7 +211,18 @@
             for copy in down_copies:
                 copy.wait_send()
 
-    start_up(up[:1])
+    edge = sub == n_sub - 1
+    place = lax.rem(col, 2 * side)
+    leads = edge & (place == 2 * side - 1)
+    yields = edge & (place == 2 * side - 2)
+
+    @pl.when(has_next & jnp.logical_not(yields))
+    def _():
+        up[0].start()
+
+    @pl.when(has_next & leads)
+    def _():
+        up[1].start()
 
     signal(known.at[0], along(1))
 
@@ -273,7 +290,17 @@
     ]
     for copy in z_copies:
         copy.start()
-    start_up([coef_up] + up[1:])
+    @pl.when(has_next & yields)
+    def _():
+        up[0].start()
+
+    start_up([coef_up])
+
+    @pl.when(has_next & jnp.logical_not(leads))
+    def _():
+        up[1].start()
+
+    start_up(up[2:])
     start_down([coef_down] + down[1:])
     keep_z = pltpu.make_async_copy(zsend, zbuf.at[sub], load_sem.at[10])
     keep_z.start()
@@ -295,10 +322,10 @@
         packed[leaf] = jnp.concatenate([blocks[leaf, k, :, rows_a:rows] for k in range(1, near)], axis=1)
         return carry
 
-    lax.fori_loop(0, leaves // 2, own_product, 0)
+    lax.fori_loop(0, leaves // 2, own_product, 0, unroll=2)
     pl.semaphore_wait(known.at[6], 2)
     tell(7, (along(4), along(-4)))
-    lax.fori_loop(leaves // 2, leaves, own_product, 0)
+    lax.fori_loop(leaves // 2, leaves, own_product, 0, unroll=2)
     pl.semaphore_wait(known.at[7], 2)
     tell(8, (along(8), along(-8)))
 
@@ -350,7 +377,7 @@
         field[leaf] = matmul(left, right)
         return carry
 
-    lax.fori_loop(0, leaves, far_sum, 0)
+    lax.fori_loop(0, leaves, far_sum, 0, unroll=4)
 
     keep_t.wait()
     lax.fori_loop(1, n_col, wait_top, 0)
@@ -365,11 +392,11 @@
         acc[leaf] += matmul_t(basis[leaf], value.astype(BF))
         return carry
 
-    lax.fori_loop(0, leaves, far_product, 0)
+    lax.fori_loop(0, leaves, far_product, 0, unroll=4)
 
     for load in window_loads:
         load.wait()
-    finish(up[:2], down[:2])
+    finish(up[:3], down[:3])
 
     def near_first(leaf, carry):
         value = acc[leaf]
@@ -378,8 +405,8 @@
         acc[leaf] = value
         return carry
 
-    lax.fori_loop(0, leaves, near_first, 0)
-    finish(up[2:], down[2:])
+    lax.fori_loop(0, leaves, near_first, 0, unroll=4)
+    finish(up[3:], down[3:])
 
     def near_second(leaf, carry):
         right = jnp.concatenate([win_b[within(near_index[k, leaf])] for k in range(1, near)], axis=0)
@@ -413,7 +440,7 @@
     scalars = anywhere
     dma = pltpu.SemaphoreType.DMA
     out = pl.pallas_call(
-        functools.partial(kernel, n_col, n_sub, math.isqrt(n_col // 2), 4),
+        functools.partial(kernel, n_col, n_sub, math.isqrt(n_col // 2), 5, 3),
         out_shape=pltpu.VMEM((leaves, rows, cols), BF),
         in_specs=[
             anywhere,
@@ -451,8 +478,8 @@
             pltpu.VMEM((leaves, rank, cols), F32),
             pltpu.VMEM((leaves, rows, cols), F32),
             dma((11,)),
-            dma((6,)),
-            dma((6,)),
+            dma((8,)),
+            dma((8,)),
             dma((2,)),
             dma((2,)),
             dma((n_sub,)),

time: 39.6 us -> 38.4 us (0.970)
  the two profiles are of different devices: /device:TPU:3 before, /device:TPU:1 now
where the time goes in v4:
time: 38.4 us; the launch traced here: 38.3 us
  Pallas kernels  37.3 us (97%)
  local copies, waits for them, and re-layouts  0.97 us (3%)
    pallas_call x1, Pallas kernels, local(): pl.pallas_call(functools.partial(kernel, n_col, n_sub, math.isqrt(n_col /...  37.3 us
    unnamed x1, local copies, waits for them, and re-layouts  0.97 us

profile of v4, /device:TPU:1, one launch (start us, length us, event | category | flops | bytes accessed | tf_op | source)
XLA Modules:
  0.0 38.3 jit_solution(7545083429712596886)
XLA Ops:
  0.0 37.3 %shard_map.118 = bf16[16,256,128]{2,1,0:T(8,128)(2,1)S(1)} custom-call(bf16[16,256,128]{2,1,0:T(8,128)(2,1)} %bitcast.5, bf16[16,4,256,256]{3,2,1,0:T(8,128)(2,1)} %near_blocks.1, s32[4,16]{1,0:T(4,128)} %bitcast.7, bf16[16,32,256]{2,1,0:T(8,128)(2,1)} %leaf_basis.1, f32[16,32,32]{2,1,0:T(8,128)} %leaf_transfer.1, f32[16,8,32,32]{3,2,1,0:T(8,128)} %leaf_coupling.1, ...), custom_call_target="tpu_custom_call" | custom-call | tf_op jit(solution)/shard_map/pallas_call | solution.py:442
  37.4 1.0 %copy.14 = bf16[4096,128]{1,0:T(8,128)(2,1)} copy(bf16[4096,128]{1,0:T(8,128)(2,1)S(1)} %bitcast.4) | data formatting | bytes 2097152

commit v5 on v4

--- a/solution.py
+++ b/solution.py
@@ -116,7 +116,7 @@
         pl.semaphore_signal(sem, inc=1, device_id=target, device_id_type=MESH)
 
     barrier = pltpu.get_barrier_semaphore()
-    signal(barrier, along(-1))
+    signal(barrier, along(1))
 
     @pl.when(has_prev)
     def _():
@@ -213,7 +213,7 @@
 
     edge = sub == n_sub - 1
     place = lax.rem(col, 2 * side)
-    leads = edge & (place == 2 * side - 1)
+    leads = edge & ((place == 2 * side - 1) | (col == 0))
     yields = edge & (place == 2 * side - 2)
 
     @pl.when(has_next & jnp.logical_not(yields))
@@ -224,7 +224,7 @@
     def _():
         up[1].start()
 
-    signal(known.at[0], along(1))
+    signal(known.at[0], along(-1))
 
     @pl.when(has_next)
     def _():
@@ -275,6 +275,10 @@
     zsend[rank : rank + tall] = jnp.concatenate(
         [c_transfer[0, tall * q : tall * (q + 1)] for q in range(rank // tall)], axis=1
     ).astype(BF)
+
+    @pl.when(has_next & yields)
+    def _():
+        up[0].start()
 
     pl.semaphore_wait(known.at[5], 2)
     z_copies = [
@@ -290,10 +294,6 @@
     ]
     for copy in z_copies:
         copy.start()
-    @pl.when(has_next & yields)
-    def _():
-        up[0].start()
-
     start_up([coef_up])
 
     @pl.when(has_next & jnp.logical_not(leads))

time: 38.4 us -> 37.7 us (0.982)
  Pallas kernels: 37.3 us -> 36.7 us
    pallas_call x1, Pallas kernels: 37.3 us -> 36.7 us  [local(): pl.pallas_call(functools.partial(kernel, n_col, n_sub, math.isqrt(n_col /...]
where the time goes in v5:
time: 37.7 us
  Pallas kernels  36.7 us (97%)
  local copies, waits for them, and re-layouts  0.97 us (3%)
    pallas_call x1, Pallas kernels, local(): pl.pallas_call(functools.partial(kernel, n_col, n_sub, math.isqrt(n_col /...  36.7 us
    unnamed x1, local copies, waits for them, and re-layouts  0.97 us

profile of v5, /device:TPU:1, one launch (start us, length us, event | category | flops | bytes accessed | tf_op | source)
XLA Modules:
  0.0 37.7 jit_solution(4458494453236401383)
XLA Ops:
  0.0 36.7 %shard_map.118 = bf16[16,256,128]{2,1,0:T(8,128)(2,1)S(1)} custom-call(bf16[16,256,128]{2,1,0:T(8,128)(2,1)} %bitcast.5, bf16[16,4,256,256]{3,2,1,0:T(8,128)(2,1)} %near_blocks.1, s32[4,16]{1,0:T(4,128)} %bitcast.7, bf16[16,32,256]{2,1,0:T(8,128)(2,1)} %leaf_basis.1, f32[16,32,32]{2,1,0:T(8,128)} %leaf_transfer.1, f32[16,8,32,32]{3,2,1,0:T(8,128)} %leaf_coupling.1, ...), custom_call_target="tpu_custom_call" | custom-call | tf_op jit(solution)/shard_map/pallas_call | solution.py:442
  36.7 1.0 %copy.14 = bf16[4096,128]{1,0:T(8,128)(2,1)} copy(bf16[4096,128]{1,0:T(8,128)(2,1)S(1)} %bitcast.4) | data formatting | bytes 2097152

commit v6 on v5

--- a/solution.py
+++ b/solution.py
@@ -290,7 +290,7 @@
             device_id=at_sub(j),
             device_id_type=MESH,
         )
-        for j in range(1, n_sub)
+        for j in sorted(range(1, n_sub), key=lambda j: -min(j, n_sub - j))
     ]
     for copy in z_copies:
         copy.start()
@@ -392,7 +392,7 @@
         acc[leaf] += matmul_t(basis[leaf], value.astype(BF))
         return carry
 
-    lax.fori_loop(0, leaves, far_product, 0, unroll=4)
+    lax.fori_loop(0, leaves, far_product, 0, unroll=16)
 
     for load in window_loads:
         load.wait()
@@ -405,7 +405,7 @@
         acc[leaf] = value
         return carry
 
-    lax.fori_loop(0, leaves, near_first, 0, unroll=4)
+    lax.fori_loop(0, leaves, near_first, 0, unroll=8)
     finish(up[3:], down[3:])
 
     def near_second(leaf, carry):

time: 37.7 us -> 37.7 us (level)
  no operation moved by 1% of the time
where the time goes in v6:
time: 37.7 us
  Pallas kernels  36.7 us (97%)
  local copies, waits for them, and re-layouts  0.97 us (3%)
    pallas_call x1, Pallas kernels, local(): pl.pallas_call(functools.partial(kernel, n_col, n_sub, math.isqrt(n_col /...  36.7 us
    unnamed x1, local copies, waits for them, and re-layouts  0.97 us

profile of v6, /device:TPU:1, one launch (start us, length us, event | category | flops | bytes accessed | tf_op | source)
XLA Modules:
  0.0 37.7 jit_solution(14402521804440912564)
XLA Ops:
  0.0 36.7 %shard_map.118 = bf16[16,256,128]{2,1,0:T(8,128)(2,1)S(1)} custom-call(bf16[16,256,128]{2,1,0:T(8,128)(2,1)} %bitcast.5, bf16[16,4,256,256]{3,2,1,0:T(8,128)(2,1)} %near_blocks.1, s32[4,16]{1,0:T(4,128)} %bitcast.7, bf16[16,32,256]{2,1,0:T(8,128)(2,1)} %leaf_basis.1, f32[16,32,32]{2,1,0:T(8,128)} %leaf_transfer.1, f32[16,8,32,32]{3,2,1,0:T(8,128)} %leaf_coupling.1, ...), custom_call_target="tpu_custom_call" | custom-call | tf_op jit(solution)/shard_map/pallas_call | solution.py:442
  36.7 1.0 %copy.14 = bf16[4096,128]{1,0:T(8,128)(2,1)} copy(bf16[4096,128]{1,0:T(8,128)(2,1)S(1)} %bitcast.4) | data formatting | bytes 2097152
